TPU v7x, 32 devices: a whole 2x2x4 slice. The times are simulated.
32 devices in a mesh: req: 4 (over z), mlp: 8 (over y, x, core).
Axes of the slice: x: 2, y: 2, z: 4, core: 2. Of those that a mesh axis runs over, the one named last changes fastest.
Arguments:
- tokens: bfloat16 [2048, 5120], P(('req', 'mlp')), may hold values from -6 to 6
- norm_scale: float32 [5120], replicated, may hold values from 0.25 to 1.75
- gate_matrix: bfloat16 [5120, 14336], P(None, 'mlp'), may hold values from -0.078125 to 0.078125
- up_matrix: bfloat16 [5120, 14336], P(None, 'mlp'), may hold values from -0.078125 to 0.078125
- down_matrix: bfloat16 [14336, 5120], P('mlp', 'req'), may hold values from -0.046875 to 0.046875
- adapter_down_maps: bfloat16 [8, 32, 5120], P('mlp'), may hold values from -0.078125 to 0.078125
- adapter_gate_up_out: bfloat16 [2, 128, 14336], P(None, None, 'mlp'), may hold values from -1.5 to 1.5
- adapter_down_proj_in: bfloat16 [128, 14336], P(None, 'mlp'), may hold values from -0.046875 to 0.046875
- adapter_down_proj_out: bfloat16 [128, 5120], replicated, may hold values from -1.5 to 1.5
- token_adapters: int32 [2048, 1], P(('req', 'mlp')), may hold values from 0 to 7; in each aligned block of 64 rows (0 to 63, 64 to 127, ...) at most 16 rows name the same one
Outputs:
- mixed: bfloat16 [2048, 5120], P(('req', 'mlp'))
Inputs may be any that keep to these rules, and one draw needn't show every extreme that they name: `token_adapters`: among the 64 rows of one device no adapter is named by more than 16 rows, and in every draw some device has an adapter named by exactly 16 of its rows.
All inputs are finite; a program needn't handle non-finite values.
Results may differ from a plain program's by a relative error of at most 0.013.
Values may be sent and summed in bfloat16 or wider, within the bound.
A program may use at most 192 MiB of HBM per device.

v0:
```python
import jax
import jax.numpy as jnp
from jax import lax
from jax.sharding import PartitionSpec as P

CAP = 16
EPS = 1e-06


def normalize(tokens, norm_scale):
    widened = tokens.astype(jnp.float32)
    mean_square = jnp.mean(widened * widened, axis=-1, keepdims=True)
    return (widened * lax.rsqrt(mean_square + EPS) * norm_scale).astype(jnp.bfloat16)


def rank_routed(normed_input, adapter_lookup, adapter_down_maps, owner_list):
    capacity = CAP
    chosen = (adapter_lookup[:, None] == jnp.arange(owner_list, dtype=jnp.int32)[None, :]).astype(
        jnp.int32
    )
    earlier = jnp.cumsum(chosen, axis=0) - chosen
    slot_of = jnp.sum(earlier * chosen, axis=1)
    target = adapter_lookup * capacity + slot_of
    dispatch = (
        jnp.arange(owner_list * capacity, dtype=jnp.int32)[:, None] == target[None, :]
    ).astype(jnp.bfloat16)
    outgoing = jnp.dot(dispatch, normed_input, preferred_element_type=jnp.float32).astype(
        jnp.bfloat16
    )
    outgoing = outgoing.reshape(owner_list, capacity, normed_input.shape[1])
    owner_table = adapter_down_maps[0]
    produced = jnp.einsum(
        "nkd,rd->nkr",
        lax.all_to_all(outgoing, "mlp", split_axis=0, concat_axis=0, tiled=True),
        owner_table,
        preferred_element_type=jnp.float32,
    ).astype(jnp.bfloat16)
    returned = lax.all_to_all(produced, "mlp", split_axis=0, concat_axis=0, tiled=True)
    returned = returned.reshape(owner_list * capacity, returned.shape[2])
    return lax.dot_general(
        dispatch, returned, (((0,), (0,)), ((), ())), preferred_element_type=jnp.float32
    ).astype(jnp.bfloat16)


def per_device(
    tokens,
    norm_scale,
    gate_matrix,
    up_matrix,
    down_matrix,
    adapter_down_maps,
    adapter_gate_up_out,
    adapter_down_proj_in,
    adapter_down_proj_out,
    token_adapters,
):
    owner_list = lax.axis_size("mlp")
    rank_span = adapter_down_maps.shape[1]
    half_rank = rank_span // 2
    normed_input = normalize(tokens, norm_scale)
    adapter_lookup = token_adapters[:, 0]
    gathered = lax.all_gather(normed_input, "mlp", axis=0, tiled=True)
    group_of = lax.all_gather(adapter_lookup, "mlp", axis=0, tiled=True)
    group_rows = gathered.shape[0]
    selector = group_of[:, None] == jnp.arange(owner_list, dtype=jnp.int32)[None, :]
    zero_half = jnp.zeros((), jnp.bfloat16)
    rank_per_token = rank_routed(normed_input, adapter_lookup, adapter_down_maps, owner_list)
    rank_rows = lax.all_gather(rank_per_token, "mlp", axis=0, tiled=True)
    spread = jnp.where(selector[:, :, None], rank_rows[:, None, :], zero_half)
    gate_rank_values = spread[:, :, :half_rank].reshape(group_rows, owner_list * half_rank)
    up_rank_values = spread[:, :, half_rank:].reshape(group_rows, owner_list * half_rank)
    gate_total = jnp.dot(gathered, gate_matrix, preferred_element_type=jnp.float32) + jnp.dot(
        gate_rank_values, adapter_gate_up_out[0], preferred_element_type=jnp.float32
    )
    up_total = jnp.dot(gathered, up_matrix, preferred_element_type=jnp.float32) + jnp.dot(
        up_rank_values, adapter_gate_up_out[1], preferred_element_type=jnp.float32
    )
    hidden_state = (jax.nn.silu(gate_total) * up_total).astype(jnp.bfloat16)
    rank_term = lax.dot_general(
        hidden_state,
        adapter_down_proj_in,
        (((1,), (1,)), ((), ())),
        preferred_element_type=jnp.float32,
    )
    picker = jnp.repeat(selector, half_rank, axis=1)
    rank_term = jnp.where(picker, rank_term, jnp.float32(0.0))
    down_term = jnp.dot(
        hidden_state,
        lax.all_gather(down_matrix, "req", axis=1, tiled=True),
        preferred_element_type=jnp.float32,
    )
    projected_down = lax.psum_scatter(
        down_term.astype(jnp.bfloat16), "mlp", scatter_dimension=0, tiled=True
    ).astype(jnp.float32)
    total_rank = lax.psum_scatter(
        rank_term.astype(jnp.bfloat16), "mlp", scatter_dimension=0, tiled=True
    )
    adapter_down_term = jnp.dot(
        total_rank, adapter_down_proj_out, preferred_element_type=jnp.float32
    )
    return (tokens.astype(jnp.float32) + projected_down + adapter_down_term).astype(jnp.bfloat16)


def solution(mesh):
    return jax.shard_map(
        per_device,
        mesh=mesh,
        in_specs=(
            P(("req", "mlp"), None),
            P(),
            P(None, "mlp"),
            P(None, "mlp"),
            P("mlp", "req"),
            P("mlp", None, None),
            P(None, None, "mlp"),
            P(None, "mlp"),
            P(),
            P(("req", "mlp"), None),
        ),
        out_specs=P(("req", "mlp"), None),
        check_vma=False,
    )
```

profile of v0, /device:TPU:0, one launch (start us, length us, event | category | flops | bytes accessed | tf_op | source)
XLA Modules:
  0.0 487.8 jit_solution(2720626967359429223)
XLA Ops:
  6.5 1.4 fusion.1
  8.0 2.2 fusion.3
  10.2 0.7 all-gather.7.cloned.1.call-update
  11.0 0.1 fusion.15
  11.0 0.1 reduce_window_sum.11
  11.1 0.6 dynamic-slice
  12.4 0.2 select_reduce_fusion
  12.6 0.1 multiply_add_fusion
  12.7 1.5 convolution_convert_fusion.1
  14.2 5.2 %all-to-all-start = ((bf16[8,16,5120]{2,1,0:T(8,128)(2,1)}), bf16[8,16,5120]{2,1,0:T(8,128)(2,1)S(1)}, u32[]{:S(2)}, u32[]{:S(2)}) async-start(bf16[8,16,5120]{2,1,0:T(8,128)(2,1)} %bitcast.2), calls=%async_computation | async-start | bytes 2621440 | tf_op jit(solution)/shard_map/all_to_all | solution.py:34
  19.4 27.4 %all-reduce = s32[512]{0:T(512)S(1)} all-reduce(s32[512]{0:T(512)S(1)} %get-tuple-element.8), channel_id=2, replica_groups=mesh['req'=4,'mlp'=8] {'mlp'}, use_global_device_ids=true, to_apply=%add | all-reduce | flops 512 | bytes 4096
  46.9 2.1 convolution_convert_fusion.2
  48.9 1.5 reshape.71
  50.4 3.3 all-to-all-start.1
  53.6 0.0 reduce-scatter.7.cloned.1.call-start
  53.7 0.1 copy.13
  53.9 4.5 all-to-all-done.1
  58.3 0.1 reshape.72
  58.4 0.2 fusion.5
  58.6 8.4 %all-gather.1 = bf16[8,64,32]{1,2,0:T(8,128)(2,1)S(1)} all-gather(bf16[1,64,32]{1,2,0:T(8,128)(2,1)S(1)} %fusion.5), channel_id=1, replica_groups=mesh['req'=4,'mlp'=8] {'mlp'}, dimensions={0}, use_global_device_ids=true | all-gather | bytes 36864 | tf_op jit(solution)/shard_map/all_gather | solution.py:68
  67.1 0.1 reshape.64
  67.3 2.6 fusion.6
  69.8 2.4 fusion.8
  72.3 17.4 %fusion.17 = f32[512,1792]{1,0:T(8,128)} fusion(bf16[512,5120]{1,0:T(8,128)(2,1)} %all-gather.5.cloned.1.call-done, bf16[5120,1792]{1,0:T(8,128)(2,1)} %param.12), kind=kOutput, calls=%fused_computation.35 | convolution fusion | flops 9395240960 | bytes 27262976 | tf_op jit(solution)/shard_map/dot_general | solution.py:72
  89.7 17.4 %multiply_convert_fusion = bf16[512,1792]{1,0:T(8,128)(2,1)S(1)} fusion(f32[512,1792]{1,0:T(8,128)S(1)} %copy-done.3, f32[512,1792]{1,0:T(8,128)} %fusion.17, f32[512,1792]{1,0:T(8,128)S(1)} %copy-done.4, bf16[512,5120]{1,0:T(8,128)(2,1)} %all-gather.5.cloned.1.call-done, bf16[5120,1792]{1,0:T(8,128)(2,1)} %param.13), kind=kOutput, calls=%fused_computation.4 | convolution fusion | flops 9402580992 | bytes 36438016 | tf_op jit(solution)/shard_map/dot_general | solution.py:75
  107.1 1.3 fusion.4
  108.4 0.3 reduce-scatter.5.cloned.1.call-start
  108.7 274.7 %all-gather.7.cloned.1.call-done = bf16[1792,5120]{1,0:T(8,128)(2,1)} async-done(((bf16[1792,1280]{1,0:T(8,128)(2,1)}), bf16[1792,5120]{1,0:T(8,128)(2,1)}) %all-gather.7.cloned.1.call-update) | async-done | bytes 18350096 | tf_op jit(solution)/shard_map/all_gather | solution.py:89
  383.4 15.0 %convolution_convert_fusion = bf16[512,5120]{1,0:T(8,128)(2,1)} fusion(bf16[512,1792]{1,0:T(8,128)(2,1)S(1)} %multiply_convert_fusion, bf16[1792,5120]{1,0:T(8,128)(2,1)} %all-gather.7.cloned.1.call-done), kind=kOutput, calls=%fused_computation | convolution fusion | flops 9397862400 | bytes 25427968 | tf_op jit(solution)/shard_map/dot_general | solution.py:87
  398.4 20.3 %reduce-scatter.7.cloned.1.call-done = bf16[64,128]{1,0:T(8,128)(2,1)} async-done(((bf16[512,128]{1,0:T(8,128)(2,1)}), bf16[64,128]{1,0:T(8,128)(2,1)}) %reduce-scatter.7.cloned.1.call-update) | async-done | bytes 16400
  418.7 60.3 %reduce-scatter.5.cloned.1.call-done = bf16[64,5120]{1,0:T(8,128)(2,1)} async-done(((bf16[512,5120]{1,0:T(8,128)(2,1)}), bf16[64,5120]{1,0:T(8,128)(2,1)}) %reduce-scatter.5.cloned.1.call-update) | async-done | bytes 655376 | tf_op jit(solution)/shard_map/reduce_scatter | solution.py:92
  479.0 2.3 fusion
  (32 shorter events, 0.2 us)
Async XLA Ops:
  6.5 472.4 %copy-start = (bf16[128,5120]{1,0:T(8,128)(2,1)S(1)}, bf16[128,5120]{1,0:T(8,128)(2,1)}, u32[]{:S(2)}) copy-start(bf16[128,5120]{1,0:T(8,128)(2,1)} %param.18) | copy-start | bytes 3932164
  6.5 4.6 copy-start.8
  6.5 4.4 copy-start.7
  6.5 65.7 %all-gather.5.cloned.1.call-start = ((), (), s32[]{:S(2)}) async-start(), calls=%async_computation.4 | async-start | bytes 5898240 | tf_op jit(solution)/shard_map/all_gather | solution.py:62
  10.2 2.5 copy-start.1
  10.2 373.2 %all-gather.7.cloned.1.call-start = ((), (), s32[]{:S(2)}) async-start(), calls=%async_computation.5 | async-start | bytes 22937600 | tf_op jit(solution)/shard_map/all_gather | solution.py:89
  12.7 54.6 %copy-start.5 = (bf16[2,128,1792]{2,1,0:T(8,128)(2,1)S(1)}, bf16[2,128,1792]{2,1,0:T(8,128)(2,1)}, u32[]{:S(2)}) copy-start(bf16[2,128,1792]{2,1,0:T(8,128)(2,1)} %param.16) | copy-start | bytes 2752516
  14.2 32.6 %all-to-all-start = ((bf16[8,16,5120]{2,1,0:T(8,128)(2,1)}), bf16[8,16,5120]{2,1,0:T(8,128)(2,1)S(1)}, u32[]{:S(2)}, u32[]{:S(2)}) async-start(bf16[8,16,5120]{2,1,0:T(8,128)(2,1)} %bitcast.2), calls=%async_computation | async-start | bytes 2621440 | tf_op jit(solution)/shard_map/all_to_all | solution.py:34
  50.4 8.0 %all-to-all-start.1 = ((bf16[8,2,256]{2,1,0:T(2,128)(2,1)}), bf16[8,2,256]{2,1,0:T(2,128)(2,1)S(1)}, u32[]{:S(2)}, u32[]{:S(2)}) async-start(bf16[8,2,256]{2,1,0:T(2,128)(2,1)} %reshape.71), calls=%async_computation.1 | async-start | bytes 16384 | tf_op jit(solution)/shard_map/all_to_all | solution.py:38
  53.6 365.0 %reduce-scatter.7.cloned.1.call-start = ((), (), s32[]{:S(2)}) async-start(), calls=%async_computation.7 | async-start | bytes 147456
  72.3 17.4 %copy-start.3 = (f32[512,1792]{1,0:T(8,128)S(1)}, f32[512,1792]{1,0:T(8,128)}, u32[]{:S(2)}) copy-start(f32[512,1792]{1,0:T(8,128)} %fusion.6) | copy-start | bytes 11010052
  72.3 17.4 %copy-start.4 = (f32[512,1792]{1,0:T(8,128)S(1)}, f32[512,1792]{1,0:T(8,128)}, u32[]{:S(2)}) copy-start(f32[512,1792]{1,0:T(8,128)} %fusion.8) | copy-start | bytes 11010052
  89.7 17.4 %copy-start.6 = (bf16[128,1792]{1,0:T(8,128)(2,1)S(1)}, bf16[128,1792]{1,0:T(8,128)(2,1)}, u32[]{:S(2)}) copy-start(bf16[128,1792]{1,0:T(8,128)(2,1)} %param.17) | copy-start | bytes 1376260
  108.4 370.5 %reduce-scatter.5.cloned.1.call-start = ((), (), s32[]{:S(2)}) async-start(), calls=%async_computation.6 | async-start | bytes 5898240 | tf_op jit(solution)/shard_map/reduce_scatter | solution.py:92
  398.4 80.6 %copy-start.2 = (bf16[64,5120]{1,0:T(8,128)(2,1)S(1)}, bf16[64,5120]{1,0:T(8,128)(2,1)}, u32[]{:S(2)}) copy-start(bf16[64,5120]{1,0:T(8,128)(2,1)} %param.10) | copy-start | bytes 1966084
Sparse Core Ops, SparseCore 0:
  10.3 57.3 all-gather.4
  69.3 314.0 all-gather.6
  386.4 32.2 reduce-scatter.6
  422.3 56.6 reduce-scatter.4
where the time goes:
time: 488 us
  waiting for transfers between devices  360 us (74%)
  matrix products  62.2 us (13%)
  blocking collectives  35.9 us (7%)
  between operations  13.9 us (3%)
  starting transfers between devices  8.78 us (2%)
    all_gather x1, waiting for transfers between devices, per_device(): lax.all_gather(down_matrix, 'req', axis=1, tiled=True)  275 us
    reduce_scatter x1, waiting for transfers between devices, per_device(): lax.psum_scatter(down_term.astype(jnp.bfloat16), 'mlp', scatter_dimension...  60.3 us
    unnamed x1, blocking collectives  27.4 us
    unnamed x5, waiting for transfers between devices  21 us
    dot_general x1, matrix products, per_device(): jnp.dot(gathered, gate_matrix, preferred_element_type=jnp.float32)  17.4 us
    dot_general x1, matrix products, per_device(): jnp.dot(gathered, up_matrix, preferred_element_type=jnp.float32)  17.4 us
    dot_general x1, matrix products, per_device(): jnp.dot(hidden_state, lax.all_gather(down_matrix, 'req', axis=1, tiled=Tr...  15 us
  transfers between devices with their start and end apart: 6, of which 4 were waited for; matrix products, arithmetic and copies ran while one was open for 13% of the time, Pallas kernels for 0%

commit v1 on v0

--- a/solution.py
+++ b/solution.py
@@ -5,6 +5,24 @@
 
 CAP = 16
 EPS = 1e-06
+
+
+def ring_gather(value, axis, dim):
+    ways, here, hop = (lax.axis_size(axis), lax.axis_index(axis), value.shape[dim])
+    lengths = [n * ways if d == dim else n for d, n in enumerate(value.shape)]
+    full = lax.dynamic_update_slice_in_dim(
+        jnp.zeros(lengths, value.dtype), value, here * hop, axis=dim
+    )
+    going_up = going_down = value
+    for far in range(1, ways // 2 + 1):
+        going_up = lax.ppermute(going_up, axis, [(d, (d + 1) % ways) for d in range(ways)])
+        full = lax.dynamic_update_slice_in_dim(full, going_up, (here - far) % ways * hop, axis=dim)
+        if 2 * far < ways:
+            going_down = lax.ppermute(going_down, axis, [(d, (d - 1) % ways) for d in range(ways)])
+            full = lax.dynamic_update_slice_in_dim(
+                full, going_down, (here + far) % ways * hop, axis=dim
+            )
+    return full
 
 
 def normalize(tokens, norm_scale):
@@ -85,9 +103,7 @@
     picker = jnp.repeat(selector, half_rank, axis=1)
     rank_term = jnp.where(picker, rank_term, jnp.float32(0.0))
     down_term = jnp.dot(
-        hidden_state,
-        lax.all_gather(down_matrix, "req", axis=1, tiled=True),
-        preferred_element_type=jnp.float32,
+        hidden_state, ring_gather(down_matrix, "req", 1), preferred_element_type=jnp.float32
     )
     projected_down = lax.psum_scatter(
         down_term.astype(jnp.bfloat16), "mlp", scatter_dimension=0, tiled=True

time: 488 us -> 396 us (0.81)
  waiting for transfers between devices: 360 us -> 243 us
  local copies, waits for them, and re-layouts: 2.53 us -> 26.8 us
  blocking collectives: 35.9 us -> 29.5 us
    all_gather x1 -> x0, waiting for transfers between devices: 275 us -> none  [per_device(): lax.all_gather(down_matrix, 'req', axis=1, tiled=True)]
    ppermute x0 -> x3, waiting for transfers between devices: none -> 184 us  [the longest x1 92.3 us: ring_gather(): lax.ppermute(going_down, axis, [(d, (d - 1) % ways) for d in range(ways)])]
    unnamed x5 -> x4, waiting for transfers between devices: 21 us -> 0.07 us
    dynamic_update_slice x0 -> x4, local copies, waits for them, and re-layouts: none -> 17.1 us  [the longest x2 9.64 us: ring_gather(): lax.dynamic_update_slice_in_dim(full, going_up, (here - far) % ways * hop...]
    broadcast_in_dim x0 -> x1, local copies, waits for them, and re-layouts: none -> 7.3 us  [ring_gather(): jnp.zeros(lengths, value.dtype)]
    unnamed x1, blocking collectives: 27.4 us -> 21.2 us
    reduce_scatter x1, waiting for transfers between devices: 60.3 us -> 55 us  [per_device(): lax.psum_scatter(down_term.astype(jnp.bfloat16), 'mlp', scatter_dimension...]
    ppermute x0 -> x3, starting transfers between devices: none -> 5.17 us  [the longest x2 3.08 us: ring_gather(): lax.ppermute(going_up, axis, [(d, (d + 1) % ways) for d in range(ways)])]
  transfers between devices with their start and end apart: 6 -> 8, of which waited for: 4 -> 5; matrix products, arithmetic and copies ran while one was open for 13% -> 23% of each run, Pallas kernels for 0% -> 0%
where the time goes in v1:
time: 396 us
  waiting for transfers between devices  243 us (61%)
  matrix products  61.3 us (15%)
  blocking collectives  29.5 us (7%)
  local copies, waits for them, and re-layouts  26.8 us (7%)
  between operations  14 us (4%)
  starting transfers between devices  12.8 us (3%)
  other arithmetic  8.13 us (2%)
    ppermute x1, waiting for transfers between devices, ring_gather(): lax.ppermute(going_down, axis, [(d, (d - 1) % ways) for d in range(ways)])  92.3 us
    ppermute x2, waiting for transfers between devices, ring_gather(): lax.ppermute(going_up, axis, [(d, (d + 1) % ways) for d in range(ways)])  91.7 us
    reduce_scatter x1, waiting for transfers between devices, per_device(): lax.psum_scatter(down_term.astype(jnp.bfloat16), 'mlp', scatter_dimension...  55 us
    unnamed x1, blocking collectives  21.2 us
    dot_general x1, matrix products, per_device(): jnp.dot(gathered, up_matrix, preferred_element_type=jnp.float32)  17.3 us
    dot_general x1, matrix products, per_device(): jnp.dot(gathered, gate_matrix, preferred_element_type=jnp.float32)  16.2 us
    dot_general x1, matrix products, per_device(): jnp.dot(hidden_state, ring_gather(down_matrix, 'req', 1), preferred_eleme...  14.9 us
    dynamic_update_slice x2, local copies, waits for them, and re-layouts, ring_gather(): lax.dynamic_update_slice_in_dim(full, going_up, (here - far) % ways * hop...  9.64 us
  transfers between devices with their start and end apart: 8, of which 5 were waited for; matrix products, arithmetic and copies ran while one was open for 23% of the time, Pallas kernels for 0%

profile of v1, /device:TPU:0, one launch (start us, length us, event | category | flops | bytes accessed | tf_op | source)
XLA Modules:
  0.0 395.8 jit_solution(16940935980259489717)
XLA Ops:
  6.5 1.4 fusion
  8.0 2.2 fusion.2
  10.2 3.1 collective-permute-start
  13.2 2.1 collective-permute-start.1
  15.3 0.7 fusion.16
  16.1 1.3 dynamic-slice
  18.1 0.8 select_reduce_fusion
  18.9 0.7 multiply_add_fusion
  19.6 2.7 convolution_convert_fusion.1
  22.4 4.0 %all-to-all-start = ((bf16[8,16,5120]{2,1,0:T(8,128)(2,1)}), bf16[8,16,5120]{2,1,0:T(8,128)(2,1)S(1)}, u32[]{:S(2)}, u32[]{:S(2)}) async-start(bf16[8,16,5120]{2,1,0:T(8,128)(2,1)} %bitcast.2), calls=%async_computation | async-start | bytes 2621440 | tf_op jit(solution)/shard_map/all_to_all | solution.py:52
  26.4 21.2 %all-reduce = s32[512]{0:T(512)S(1)} all-reduce(s32[512]{0:T(512)S(1)} %get-tuple-element.8), channel_id=2, replica_groups=mesh['req'=4,'mlp'=8] {'mlp'}, use_global_device_ids=true, to_apply=%add | all-reduce | flops 512 | bytes 4096
  47.6 7.3 %broadcast_in_dim.42 = bf16[1792,5120]{1,0:T(8,128)(2,1)} broadcast(bf16[]{:T(256)} %constant.47.clone.1), dimensions={} | broadcast | bytes 18350082 | tf_op jit(solution)/shard_map/broadcast_in_dim | solution.py:14
  54.9 2.6 constant_dynamic-update-slice_fusion.3
  58.0 0.7 reshape.71
  58.7 3.3 all-to-all-start.1
  62.3 4.3 %all-to-all-done.1 = bf16[8,2,256]{2,1,0:T(2,128)(2,1)S(1)} async-done(((bf16[8,2,256]{2,1,0:T(2,128)(2,1)}), bf16[8,2,256]{2,1,0:T(2,128)(2,1)S(1)}, u32[]{:S(2)}, u32[]{:S(2)}) %all-to-all-start.1) | async-done | bytes 8224 | tf_op jit(solution)/shard_map/all_to_all | solution.py:56
  66.9 8.3 %all-gather.1 = bf16[8,64,32]{1,2,0:T(8,128)(2,1)S(1)} all-gather(bf16[1,64,32]{1,2,0:T(8,128)(2,1)S(1)} %fusion.6), channel_id=1, replica_groups=mesh['req'=4,'mlp'=8] {'mlp'}, dimensions={0}, use_global_device_ids=true | all-gather | bytes 36864 | tf_op jit(solution)/shard_map/all_gather | solution.py:86
  75.4 3.5 fusion.7
  78.9 3.5 fusion.9
  82.4 33.0 %collective-permute-done = bf16[1792,1280]{1,0:T(8,128)(2,1)} collective-permute-done((bf16[1792,1280]{1,0:T(8,128)(2,1)}, bf16[1792,1280]{1,0:T(8,128)(2,1)}, u32[]{:S(2)}, u32[]{:S(2)}) %collective-permute-start) | collective-permute-done | bytes 4587552 | tf_op jit(solution)/shard_map/ppermute | solution.py:18
  115.4 4.8 %constant_dynamic-update-slice_fusion.2 = bf16[1792,5120]{1,0:T(8,128)(2,1)} fusion(bf16[1792,5120]{1,0:T(8,128)(2,1)} %constant_dynamic-update-slice_fusion.3, bf16[1792,1280]{1,0:T(8,128)(2,1)} %collective-permute-done, s32[]{:T(128)S(6)} %select_n.38), kind=kLoop, calls=%fused_computation.33 | loop fusion | bytes 9175044 | tf_op jit(solution)/shard_map/dynamic_update_slice | solution.py:19
  120.3 92.3 %collective-permute-done.1 = bf16[1792,1280]{1,0:T(8,128)(2,1)} collective-permute-done((bf16[1792,1280]{1,0:T(8,128)(2,1)}, bf16[1792,1280]{1,0:T(8,128)(2,1)}, u32[]{:S(2)}, u32[]{:S(2)}) %collective-permute-start.1) | collective-permute-done | bytes 4587552 | tf_op jit(solution)/shard_map/ppermute | solution.py:21
  212.5 4.9 %constant_dynamic-update-slice_fusion.1 = bf16[1792,5120]{1,0:T(8,128)(2,1)} fusion(bf16[1792,5120]{1,0:T(8,128)(2,1)} %constant_dynamic-update-slice_fusion.2, bf16[1792,1280]{1,0:T(8,128)(2,1)} %collective-permute-done.1, s32[]{:T(128)S(6)} %select_n.40), kind=kLoop, calls=%fused_computation.32 | loop fusion | bytes 9175044 | tf_op jit(solution)/shard_map/dynamic_update_slice | solution.py:22
  217.4 16.2 %fusion.18 = f32[512,1792]{1,0:T(8,128)} fusion(bf16[512,5120]{1,0:T(8,128)(2,1)} %all-gather.4.cloned.1.call-done, bf16[5120,1792]{1,0:T(8,128)(2,1)} %param.12), kind=kOutput, calls=%fused_computation.39 | convolution fusion | flops 9395240960 | bytes 27262976 | tf_op jit(solution)/shard_map/dot_general | solution.py:90
  233.7 17.3 %multiply_convert_fusion = bf16[512,1792]{1,0:T(8,128)(2,1)S(1)} fusion(f32[512,1792]{1,0:T(8,128)S(1)} %copy-done.2, f32[512,1792]{1,0:T(8,128)} %fusion.18, f32[512,1792]{1,0:T(8,128)S(1)} %copy-done.3, bf16[512,5120]{1,0:T(8,128)(2,1)} %all-gather.4.cloned.1.call-done, bf16[5120,1792]{1,0:T(8,128)(2,1)} %param.13), kind=kOutput, calls=%fused_computation.2 | convolution fusion | flops 9402580992 | bytes 36438016 | tf_op jit(solution)/shard_map/dot_general | solution.py:93
  251.0 1.3 fusion.5
  252.6 58.7 %collective-permute-done.2 = bf16[1792,1280]{1,0:T(8,128)(2,1)} collective-permute-done((bf16[1792,1280]{1,0:T(8,128)(2,1)}, bf16[1792,1280]{1,0:T(8,128)(2,1)}, u32[]{:S(2)}, u32[]{:S(2)}) %collective-permute-start.2) | collective-permute-done | bytes 4587552 | tf_op jit(solution)/shard_map/ppermute | solution.py:18
  311.2 4.8 %constant_dynamic-update-slice_fusion = bf16[1792,5120]{1,0:T(8,128)(2,1)} fusion(bf16[1792,5120]{1,0:T(8,128)(2,1)} %constant_dynamic-update-slice_fusion.1, bf16[1792,1280]{1,0:T(8,128)(2,1)} %collective-permute-done.2, s32[]{:T(128)S(6)} %select_n.42), kind=kLoop, calls=%fused_computation.31 | loop fusion | bytes 9175044 | tf_op jit(solution)/shard_map/dynamic_update_slice | solution.py:19
  316.1 14.9 %convolution_convert_fusion = bf16[512,5120]{1,0:T(8,128)(2,1)} fusion(bf16[512,1792]{1,0:T(8,128)(2,1)S(1)} %multiply_convert_fusion, bf16[1792,5120]{1,0:T(8,128)(2,1)} %constant_dynamic-update-slice_fusion), kind=kOutput, calls=%fused_computation | convolution fusion | flops 9397862400 | bytes 25427968 | tf_op jit(solution)/shard_map/dot_general | solution.py:105
  331.0 1.1 fusion.19
  332.1 55.0 %reduce-scatter.5.cloned.1.call-done = bf16[64,5120]{1,0:T(8,128)(2,1)} async-done(((bf16[512,5120]{1,0:T(8,128)(2,1)}), bf16[64,5120]{1,0:T(8,128)(2,1)}) %reduce-scatter.5.cloned.1.call-update) | async-done | bytes 655376 | tf_op jit(solution)/shard_map/reduce_scatter | solution.py:108
  387.1 2.1 fusion.4
  (40 shorter events, 1.6 us)
Async XLA Ops:
  6.5 324.5 %copy-start = (bf16[128,5120]{1,0:T(8,128)(2,1)S(1)}, bf16[128,5120]{1,0:T(8,128)(2,1)}, u32[]{:S(2)}) copy-start(bf16[128,5120]{1,0:T(8,128)(2,1)} %param.18) | copy-start | bytes 3932164
  6.5 210.9 %all-gather.4.cloned.1.call-start = ((), (), s32[]{:S(2)}) async-start(), calls=%async_computation.4 | async-start | bytes 5898240 | tf_op jit(solution)/shard_map/all_gather | solution.py:80
  10.2 105.3 %collective-permute-start = (bf16[1792,1280]{1,0:T(8,128)(2,1)}, bf16[1792,1280]{1,0:T(8,128)(2,1)}, u32[]{:S(2)}, u32[]{:S(2)}) collective-permute-start(bf16[1792,1280]{1,0:T(8,128)(2,1)} %param.14), channel_id=1, source_target_pairs={{0,8},{8,16},{16,24},{24,0},{1,9},{9,17},{17,25},{25,1},{2,10},{10... | collective-permute-start | bytes 13762568 | tf_op jit(solution)/shard_map/ppermute | solution.py:18
  13.2 199.3 %collective-permute-start.1 = (bf16[1792,1280]{1,0:T(8,128)(2,1)}, bf16[1792,1280]{1,0:T(8,128)(2,1)}, u32[]{:S(2)}, u32[]{:S(2)}) collective-permute-start(bf16[1792,1280]{1,0:T(8,128)(2,1)} %param.14), channel_id=1, source_target_pairs={{0,24},{8,0},{16,8},{24,16},{1,25},{9,1},{17,9},{25,17},{2,26},{10... | collective-permute-start | bytes 13762568 | tf_op jit(solution)/shard_map/ppermute | solution.py:21
  22.4 32.5 %slice-start = ((s8[4587520]{0:T(1024)(128)(4,1)}), s8[393216]{0:T(1024)(128)(4,1)S(1)}, s32[]{:S(2)}) async-start(s8[4587520]{0:T(1024)(128)(4,1)} %bitcast.39), calls=%async_computation.7 | async-start | bytes 786432
  22.4 35.1 %all-to-all-start = ((bf16[8,16,5120]{2,1,0:T(8,128)(2,1)}), bf16[8,16,5120]{2,1,0:T(8,128)(2,1)S(1)}, u32[]{:S(2)}, u32[]{:S(2)}) async-start(bf16[8,16,5120]{2,1,0:T(8,128)(2,1)} %bitcast.2), calls=%async_computation | async-start | bytes 2621440 | tf_op jit(solution)/shard_map/all_to_all | solution.py:52
  47.6 7.3 %slice-start.1 = ((s8[4587520]{0:T(1024)(128)(4,1)}), s8[4194304]{0:T(1024)(128)(4,1)S(1)}, s32[]{:S(2)}) async-start(s8[4587520]{0:T(1024)(128)(4,1)} %bitcast.39), calls=%async_computation.8 | async-start | bytes 8388608
  54.9 2.6 copy-start.5
  58.7 8.0 %all-to-all-start.1 = ((bf16[8,2,256]{2,1,0:T(2,128)(2,1)}), bf16[8,2,256]{2,1,0:T(2,128)(2,1)S(1)}, u32[]{:S(2)}, u32[]{:S(2)}) async-start(bf16[8,2,256]{2,1,0:T(2,128)(2,1)} %reshape.71), calls=%async_computation.1 | async-start | bytes 16384 | tf_op jit(solution)/shard_map/all_to_all | solution.py:56
  62.0 269.0 %reduce-scatter.7.cloned.1.call-start = ((), (), s32[]{:S(2)}) async-start(), calls=%async_computation.6 | async-start | bytes 147456
  115.4 195.8 %collective-permute-start.2 = (bf16[1792,1280]{1,0:T(8,128)(2,1)}, bf16[1792,1280]{1,0:T(8,128)(2,1)}, u32[]{:S(2)}, u32[]{:S(2)}) collective-permute-start(bf16[1792,1280]{1,0:T(8,128)(2,1)} %collective-permute-done), channel_id=1, source_target_pairs={{0,8},{8,16},{16,24},{24,0},{1,9},{9,17},{17,25},{25,1},{2,10},{10... | collective-permute-start | bytes 13762568 | tf_op jit(solution)/shard_map/ppermute | solution.py:18
  217.4 16.2 %copy-start.2 = (f32[512,1792]{1,0:T(8,128)S(1)}, f32[512,1792]{1,0:T(8,128)}, u32[]{:S(2)}) copy-start(f32[512,1792]{1,0:T(8,128)} %fusion.7) | copy-start | bytes 11010052
  217.4 16.2 %copy-start.3 = (f32[512,1792]{1,0:T(8,128)S(1)}, f32[512,1792]{1,0:T(8,128)}, u32[]{:S(2)}) copy-start(f32[512,1792]{1,0:T(8,128)} %fusion.9) | copy-start | bytes 11010052
  233.6 17.3 %copy-start.4 = (bf16[128,1792]{1,0:T(8,128)(2,1)S(1)}, bf16[128,1792]{1,0:T(8,128)(2,1)}, u32[]{:S(2)}) copy-start(bf16[128,1792]{1,0:T(8,128)(2,1)} %param.17) | copy-start | bytes 1376260
  252.3 134.8 %reduce-scatter.5.cloned.1.call-start = ((), (), s32[]{:S(2)}) async-start(), calls=%async_computation.5 | async-start | bytes 5898240 | tf_op jit(solution)/shard_map/reduce_scatter | solution.py:108
  331.0 56.2 %copy-start.1 = (bf16[64,5120]{1,0:T(8,128)(2,1)S(1)}, bf16[64,5120]{1,0:T(8,128)(2,1)}, u32[]{:S(2)}) copy-start(bf16[64,5120]{1,0:T(8,128)(2,1)} %param.10) | copy-start | bytes 1966084
Sparse Core Ops, SparseCore 0:
  10.3 50.9 all-gather.3
  252.4 37.4 reduce-scatter.6
  331.1 55.9 reduce-scatter.4
